TPU v7x, 32 devices: a whole 2x2x4 slice. The times are simulated.
32 devices in a mesh: dp: 8 (over z, x), tensor: 4 (over y, core).
Axes of the slice: x: 2, y: 2, z: 4, core: 2. Of those that a mesh axis runs over, the one named last changes fastest.
Arguments:
- gradients: bfloat16 [8, 4096, 4096], P('dp', None, 'tensor'), may hold values from -300 to 300
- feedback: bfloat16 [8, 4096, 4096], P('dp', None, 'tensor'), may hold values from -12 to 12
- warm_start: float32 [4096, 64], P('tensor'), may hold values from -0.09375 to 0.09375
Outputs:
- projected: float32 [4096, 64], P('tensor')
- refreshed: float32 [4096, 64], P('tensor')
- decompressed: bfloat16 [4096, 4096], P(None, 'tensor')
All inputs are finite; a program needn't handle non-finite values.
Results may differ from a plain program's by a relative error of at most 0.001.
Values sent between devices are 32-bit elements; how exact they have to be, the bound alone decides.
A program may use at most 128 MiB of HBM per device.

v0:
```python
import jax
import jax.numpy as jnp
from jax import lax
from jax.sharding import PartitionSpec as P

HIGHEST = lax.Precision.HIGHEST


def on_device(gradients, feedback, warm_start):
    corrected = gradients[0].astype(jnp.float32) + feedback[0].astype(jnp.float32)
    members = lax.axis_size("dp")
    partial_value = lax.psum_scatter(
        jnp.dot(corrected, warm_start, precision=HIGHEST), "tensor", scatter_dimension=0, tiled=True
    )
    projected = lax.psum(partial_value, "dp") / members
    gram_matrix = lax.psum(jnp.dot(projected.T, projected, precision=HIGHEST), "tensor")
    factor = jnp.linalg.cholesky(gram_matrix)
    orth_shard = lax.linalg.triangular_solve(
        factor, projected, left_side=False, lower=True, transpose_a=True
    )
    basis = lax.all_gather(orth_shard, "tensor", axis=0, tiled=True)
    local_right = lax.dot_general(corrected, basis, (((0,), (0,)), ((), ())), precision=HIGHEST)
    refreshed = lax.psum(local_right, "dp") / members
    decompressed = jnp.dot(basis, refreshed.T, precision=HIGHEST).astype(jnp.bfloat16)
    return (projected, refreshed, decompressed)


def solution(mesh):
    return jax.shard_map(
        on_device,
        mesh=mesh,
        in_specs=(P("dp", None, "tensor"), P("dp", None, "tensor"), P("tensor", None)),
        out_specs=(P("tensor", None), P("tensor", None), P(None, "tensor")),
        check_vma=False,
    )
```

profile of v0, /device:TPU:0, one launch (start us, length us, event | category | flops | bytes accessed | tf_op | source)
XLA Modules:
  0.0 286.7 jit_solution(11949851245497997149)
XLA Ops:
  7.2 0.0 copy-start
  7.2 0.0 reduce-scatter.2.cloned.1.call-start
  7.2 0.9 copy-done
  8.1 22.3 %fusion.2 = f32[4096,64]{0,1:T(8,128)} fusion(f32[1024,64]{0,1:T(8,128)S(1)} %copy-done, bf16[1,4096,1024]{2,1,0:T(8,128)(2,1)} %param.4, bf16[1,4096,1024]{2,1,0:T(8,128)(2,1)} %param.3), kind=kOutput, calls=%fused_computation.2 | convolution fusion | flops 3233808384 | bytes 18087936 | tf_op jit(solution)/shard_map/dot_general | solution.py:13
  30.4 0.0 reduce-scatter.2.cloned.1.call-update
  30.5 0.0 all-reduce.3.cloned.1.call-start
  30.5 27.6 %reduce-scatter.2.cloned.1.call-done = f32[1024,64]{0,1:T(8,128)} async-done(((f32[4096,64]{0,1:T(8,128)}), f32[1024,64]{0,1:T(8,128)}) %reduce-scatter.2.cloned.1.call-update) | async-done | bytes 262160 | tf_op jit(solution)/shard_map/reduce_scatter | solution.py:12
  58.1 0.0 all-reduce.3.cloned.1.call-update
  58.1 0.0 all-gather.2.cloned.1.call-start
  58.2 74.3 %all-reduce.3.cloned.1.call-done = f32[1024,64]{0,1:T(8,128)} async-done(((f32[1024,64]{0,1:T(8,128)}), f32[1024,64]{0,1:T(8,128)}) %all-reduce.3.cloned.1.call-update) | async-done | bytes 262160 | tf_op jit(solution)/shard_map/psum | solution.py:15
  132.5 1.0 broadcast_multiply_fusion.1
  133.5 0.0 copy-start.2
  133.5 0.4 fusion.8
  133.9 10.3 %psum.22 = f32[64,64]{0,1:T(8,128)S(1)} all-reduce(f32[64,64]{0,1:T(8,128)S(1)} %fusion.8), channel_id=1, replica_groups=mesh['dp'=8,'tensor'=4] {'tensor'}, use_global_device_ids=true, to_apply=%region_2.0 | all-reduce | flops 4096 | bytes 32768 | tf_op jit(solution)/shard_map/psum | solution.py:16
  144.2 0.1 copy.7
  144.2 5.8 %cholesky.16 = f32[64,64]{1,0:T(8,128)S(1)} custom-call(f32[64,64]{1,0:T(8,128)S(1)} %fusion.7), custom_call_target="Cholesky" | custom-call | tf_op jit(solution)/shard_map/jit(cholesky)/cholesky | solution.py:17
  150.1 0.6 compare_reduce_fusion
  150.8 0.7 fusion.4
  151.4 4.9 %custom-call.6 = f32[1,64,64]{1,2,0:T(8,128)S(1)} custom-call(f32[1,64,64]{2,1,0:T(8,128)S(1)} %fusion.4), custom_call_target="InvertDiagBlocksLowerTriangular" | custom-call | tf_op jit(solution)/shard_map/triangular_solve | solution.py:18
  156.3 1.1 fusion.5
  157.5 0.0 all-gather.2.cloned.1.call-update
  157.5 0.2 all-reduce.5.cloned.1.call-start
  157.7 16.0 %all-gather.2.cloned.1.call-done = f32[4096,64]{0,1:T(8,128)} async-done(((f32[1024,64]{0,1:T(8,128)}), f32[4096,64]{0,1:T(8,128)}) %all-gather.2.cloned.1.call-update) | async-done | bytes 1048592 | tf_op jit(solution)/shard_map/all_gather | solution.py:21
  173.7 19.0 %fusion = f32[1024,64]{0,1:T(8,128)} fusion(f32[4096,64]{0,1:T(8,128)} %all-gather.2.cloned.1.call-done, bf16[1,4096,1024]{2,1,0:T(8,128)(2,1)} %param.4, bf16[1,4096,1024]{2,1,0:T(8,128)(2,1)} %param.3), kind=kOutput, calls=%fused_computation | convolution fusion | flops 3233808384 | bytes 18087936 | tf_op jit(solution)/shard_map/dot_general | solution.py:22
  192.7 0.0 copy-done.2
  192.7 0.0 all-reduce.5.cloned.1.call-update
  192.8 71.2 %all-reduce.5.cloned.1.call-done = f32[1024,64]{0,1:T(8,128)} async-done(((f32[1024,64]{0,1:T(8,128)}), f32[1024,64]{0,1:T(8,128)}) %all-reduce.5.cloned.1.call-update) | async-done | bytes 262160 | tf_op jit(solution)/shard_map/psum | solution.py:23
  263.9 1.0 broadcast_multiply_fusion
  264.9 0.0 copy-done.1
  264.9 0.0 copy-start.3
  264.9 15.3 %convolution_convert_fusion = bf16[4096,1024]{1,0:T(8,128)(2,1)} fusion(f32[4096,64]{0,1:T(8,128)S(1)} %copy-done.1, f32[1024,64]{0,1:T(8,128)S(1)} %broadcast_multiply_fusion), kind=kOutput, calls=%fused_computation.5 | convolution fusion | flops 3225419776 | bytes 9699328 | tf_op jit(solution)/shard_map/dot_general | solution.py:24
  280.2 0.0 copy-done.3
  (3 shorter events, 0.0 us)
Async XLA Ops:
  7.2 1.0 copy-start
  7.2 50.9 %reduce-scatter.2.cloned.1.call-start = ((), (), s32[]{:S(2)}) async-start(), calls=%async_computation.1 | async-start | bytes 1310720 | tf_op jit(solution)/shard_map/reduce_scatter | solution.py:12
  30.5 102.1 %all-reduce.3.cloned.1.call-start = ((), (), s32[]{:S(2)}) async-start(), calls=%async_computation.2 | async-start | bytes 524288 | tf_op jit(solution)/shard_map/psum | solution.py:15
  58.1 115.6 %all-gather.2.cloned.1.call-start = ((), (), s32[]{:S(2)}) async-start(), calls=%async_computation.3 | async-start | bytes 1310720 | tf_op jit(solution)/shard_map/all_gather | solution.py:21
  133.5 59.2 %copy-start.2 = (f32[1024,64]{0,1:T(8,128)}, f32[1024,64]{0,1:T(8,128)S(1)}, u32[]{:S(2)}) copy-start(f32[1024,64]{0,1:T(8,128)S(1)} %broadcast_multiply_fusion.1) | copy-start | bytes 786436
  157.5 106.4 %all-reduce.5.cloned.1.call-start = ((), (), s32[]{:S(2)}) async-start(), calls=%async_computation.4 | async-start | bytes 524288 | tf_op jit(solution)/shard_map/psum | solution.py:23
  173.7 91.2 %copy-start.1 = (f32[4096,64]{0,1:T(8,128)S(1)}, f32[4096,64]{0,1:T(8,128)}, u32[]{:S(2)}) copy-start(f32[4096,64]{0,1:T(8,128)} %all-gather.2.cloned.1.call-done) | copy-start | bytes 3145732
  264.9 15.3 %copy-start.3 = (f32[1024,64]{0,1:T(8,128)}, f32[1024,64]{0,1:T(8,128)S(1)}, u32[]{:S(2)}) copy-start(f32[1024,64]{0,1:T(8,128)S(1)} %broadcast_multiply_fusion) | copy-start | bytes 786436
Sparse Core Ops, SparseCore 0:
  30.6 27.4 reduce-scatter.1
  61.5 71.0 all-reduce.2
  157.6 16.0 all-gather.1
  192.9 71.0 all-reduce.4
where the time goes:
time: 287 us
  waiting for transfers between devices  189 us (66%)
  matrix products  58.1 us (20%)
  other arithmetic  14 us (5%)
  between operations  13.8 us (5%)
  blocking collectives  10.3 us (4%)
    psum x1, waiting for transfers between devices, on_device(): projected = lax.psum(partial_value, 'dp') / members  74.3 us
    psum x1, waiting for transfers between devices, on_device(): refreshed = lax.psum(local_right, 'dp') / members  71.2 us
    reduce_scatter x1, waiting for transfers between devices, on_device(): lax.psum_scatter(jnp.dot(corrected, warm_start, precision=HIGHEST), 'tens...  27.6 us
    dot_general x1, matrix products, on_device(): jnp.dot(corrected, warm_start, precision=HIGHEST)  22.3 us
    dot_general x1, matrix products, on_device(): lax.dot_general(corrected, basis, (((0,), (0,)), ((), ())), precision=HIG...  19 us
    all_gather x1, waiting for transfers between devices, on_device(): basis = lax.all_gather(orth_shard, 'tensor', axis=0, tiled=True)  16 us
    dot_general x1, matrix products, on_device(): jnp.dot(basis, refreshed.T, precision=HIGHEST).astype(jnp.bfloat16)  15.3 us
    psum x1, blocking collectives, on_device(): lax.psum(jnp.dot(projected.T, projected, precision=HIGHEST), 'tensor')  10.3 us
  transfers between devices with their start and end apart: 4, of which 4 were waited for; matrix products, arithmetic and copies ran while one was open for 0% of the time, Pallas kernels for 0%

commit v1 on v0

--- a/solution.py
+++ b/solution.py
@@ -20,7 +20,7 @@
     )
     basis = lax.all_gather(orth_shard, "tensor", axis=0, tiled=True)
     local_right = lax.dot_general(corrected, basis, (((0,), (0,)), ((), ())), precision=HIGHEST)
-    refreshed = lax.psum(local_right, "dp") / members
+    refreshed = jnp.sum(lax.all_gather(local_right, "dp"), axis=0) / members
     decompressed = jnp.dot(basis, refreshed.T, precision=HIGHEST).astype(jnp.bfloat16)
     return (projected, refreshed, decompressed)
 

time: 287 us -> 267 us (0.930)
  waiting for transfers between devices: 189 us -> 167 us
    psum x1 -> x0, waiting for transfers between devices: 71.2 us -> none  [on_device(): refreshed = lax.psum(local_right, 'dp') / members]
    all_gather x0 -> x1, waiting for transfers between devices: none -> 49.2 us  [on_device(): refreshed = jnp.sum(lax.all_gather(local_right, 'dp'), axis=0) / members]
where the time goes in v1:
time: 267 us
  waiting for transfers between devices  167 us (63%)
  matrix products  58.1 us (22%)
  between operations  13.9 us (5%)
  other arithmetic  13.6 us (5%)
  blocking collectives  10.3 us (4%)
  local copies, waits for them, and re-layouts  3.78 us (1%)
    psum x1, waiting for transfers between devices, on_device(): projected = lax.psum(partial_value, 'dp') / members  74.3 us
    all_gather x1, waiting for transfers between devices, on_device(): refreshed = jnp.sum(lax.all_gather(local_right, 'dp'), axis=0) / members  49.2 us
    reduce_scatter x1, waiting for transfers between devices, on_device(): lax.psum_scatter(jnp.dot(corrected, warm_start, precision=HIGHEST), 'tens...  27.6 us
    dot_general x1, matrix products, on_device(): jnp.dot(corrected, warm_start, precision=HIGHEST)  22.3 us
    dot_general x1, matrix products, on_device(): lax.dot_general(corrected, basis, (((0,), (0,)), ((), ())), precision=HIG...  19 us
    all_gather x1, waiting for transfers between devices, on_device(): basis = lax.all_gather(orth_shard, 'tensor', axis=0, tiled=True)  16 us
    dot_general x1, matrix products, on_device(): jnp.dot(basis, refreshed.T, precision=HIGHEST).astype(jnp.bfloat16)  15.3 us
    psum x1, blocking collectives, on_device(): lax.psum(jnp.dot(projected.T, projected, precision=HIGHEST), 'tensor')  10.3 us
  transfers between devices with their start and end apart: 4, of which 4 were waited for; matrix products, arithmetic and copies ran while one was open for 0% of the time, Pallas kernels for 0%

profile of v1, /device:TPU:0, one launch (start us, length us, event | category | flops | bytes accessed | tf_op | source)
XLA Modules:
  0.0 267.1 jit_solution(6046427685905476115)
XLA Ops:
  7.2 0.0 copy-start
  7.2 0.0 reduce-scatter.2.cloned.1.call-start
  7.2 0.9 copy-done
  8.1 22.3 %fusion.2 = f32[4096,64]{0,1:T(8,128)} fusion(f32[1024,64]{0,1:T(8,128)S(1)} %copy-done, bf16[1,4096,1024]{2,1,0:T(8,128)(2,1)} %param.4, bf16[1,4096,1024]{2,1,0:T(8,128)(2,1)} %param.3), kind=kOutput, calls=%fused_computation.2 | convolution fusion | flops 3233808384 | bytes 18087936 | tf_op jit(solution)/shard_map/dot_general | solution.py:13
  30.4 0.0 reduce-scatter.2.cloned.1.call-update
  30.5 0.0 all-reduce.2.cloned.1.call-start
  30.5 27.6 %reduce-scatter.2.cloned.1.call-done = f32[1024,64]{0,1:T(8,128)} async-done(((f32[4096,64]{0,1:T(8,128)}), f32[1024,64]{0,1:T(8,128)}) %reduce-scatter.2.cloned.1.call-update) | async-done | bytes 262160 | tf_op jit(solution)/shard_map/reduce_scatter | solution.py:12
  58.1 0.0 all-reduce.2.cloned.1.call-update
  58.1 0.0 all-gather.4.cloned.1.call-start
  58.2 74.3 %all-reduce.2.cloned.1.call-done = f32[1024,64]{0,1:T(8,128)} async-done(((f32[1024,64]{0,1:T(8,128)}), f32[1024,64]{0,1:T(8,128)}) %all-reduce.2.cloned.1.call-update) | async-done | bytes 262160 | tf_op jit(solution)/shard_map/psum | solution.py:15
  132.5 1.0 broadcast_multiply_fusion.1
  133.5 0.0 copy-start.2
  133.5 0.4 fusion.8
  133.9 10.3 %psum.15 = f32[64,64]{0,1:T(8,128)S(1)} all-reduce(f32[64,64]{0,1:T(8,128)S(1)} %fusion.8), channel_id=1, replica_groups=mesh['dp'=8,'tensor'=4] {'tensor'}, use_global_device_ids=true, to_apply=%region_2.0 | all-reduce | flops 4096 | bytes 32768 | tf_op jit(solution)/shard_map/psum | solution.py:16
  144.2 0.1 copy.7
  144.2 5.8 %cholesky.16 = f32[64,64]{1,0:T(8,128)S(1)} custom-call(f32[64,64]{1,0:T(8,128)S(1)} %fusion.7), custom_call_target="Cholesky" | custom-call | tf_op jit(solution)/shard_map/jit(cholesky)/cholesky | solution.py:17
  150.1 0.6 compare_reduce_fusion
  150.8 0.7 fusion.4
  151.4 4.9 %custom-call.6 = f32[1,64,64]{1,2,0:T(8,128)S(1)} custom-call(f32[1,64,64]{2,1,0:T(8,128)S(1)} %fusion.4), custom_call_target="InvertDiagBlocksLowerTriangular" | custom-call | tf_op jit(solution)/shard_map/triangular_solve | solution.py:18
  156.3 1.1 fusion.5
  157.5 0.0 all-gather.4.cloned.1.call-update
  157.5 0.2 all-gather.6.cloned.1.call-start
  157.7 16.0 %all-gather.4.cloned.1.call-done = f32[4096,64]{0,1:T(8,128)} async-done(((f32[1024,64]{0,1:T(8,128)}), f32[4096,64]{0,1:T(8,128)}) %all-gather.4.cloned.1.call-update) | async-done | bytes 1048592 | tf_op jit(solution)/shard_map/all_gather | solution.py:21
  173.7 19.0 %fusion = f32[1024,64]{0,1:T(8,128)} fusion(f32[4096,64]{0,1:T(8,128)} %all-gather.4.cloned.1.call-done, bf16[1,4096,1024]{2,1,0:T(8,128)(2,1)} %param.4, bf16[1,4096,1024]{2,1,0:T(8,128)(2,1)} %param.3), kind=kOutput, calls=%fused_computation | convolution fusion | flops 3233808384 | bytes 18087936 | tf_op jit(solution)/shard_map/dot_general | solution.py:22
  192.7 0.0 copy-done.2
  192.7 0.0 all-gather.6.cloned.1.call-update
  192.7 49.2 %all-gather.6.cloned.1.call-done = f32[8192,64]{0,1:T(8,128)} async-done(((f32[1024,64]{0,1:T(8,128)}), f32[8192,64]{0,1:T(8,128)}) %all-gather.6.cloned.1.call-update) | async-done | bytes 2097168 | tf_op jit(solution)/shard_map/all_gather | solution.py:23
  242.0 2.8 %copy.9 = f32[8,8,8,1024]{3,2,1,0:T(8,128)S(1)} copy(f32[8,8,8,1024]{3,1,2,0:T(8,128)} %bitcast.26) | data formatting | bytes 4194304
  244.7 0.5 bitcast_reduce_fusion
  245.3 0.0 copy-start.3
  245.3 15.3 %convolution_convert_fusion = bf16[4096,1024]{1,0:T(8,128)(2,1)} fusion(f32[4096,64]{0,1:T(8,128)S(1)} %copy-done.1, f32[1024,64]{0,1:T(8,128)S(1)} %broadcast_multiply_fusion), kind=kOutput, calls=%fused_computation.5 | convolution fusion | flops 3225419776 | bytes 9699328 | tf_op jit(solution)/shard_map/dot_general | solution.py:24
  260.6 0.0 copy-done.3
  (5 shorter events, 0.1 us)
Async XLA Ops:
  7.2 1.0 copy-start
  7.2 50.9 %reduce-scatter.2.cloned.1.call-start = ((), (), s32[]{:S(2)}) async-start(), calls=%async_computation.1 | async-start | bytes 1310720 | tf_op jit(solution)/shard_map/reduce_scatter | solution.py:12
  30.5 102.1 %all-reduce.2.cloned.1.call-start = ((), (), s32[]{:S(2)}) async-start(), calls=%async_computation.2 | async-start | bytes 524288 | tf_op jit(solution)/shard_map/psum | solution.py:15
  58.1 115.6 %all-gather.4.cloned.1.call-start = ((), (), s32[]{:S(2)}) async-start(), calls=%async_computation.3 | async-start | bytes 1310720 | tf_op jit(solution)/shard_map/all_gather | solution.py:21
  133.5 59.2 %copy-start.2 = (f32[1024,64]{0,1:T(8,128)}, f32[1024,64]{0,1:T(8,128)S(1)}, u32[]{:S(2)}) copy-start(f32[1024,64]{0,1:T(8,128)S(1)} %broadcast_multiply_fusion.1) | copy-start | bytes 786436
  157.5 84.5 %all-gather.6.cloned.1.call-start = ((), (), s32[]{:S(2)}) async-start(), calls=%async_computation.4 | async-start | bytes 2359296 | tf_op jit(solution)/shard_map/all_gather | solution.py:23
  173.7 71.6 %copy-start.1 = (f32[4096,64]{0,1:T(8,128)S(1)}, f32[4096,64]{0,1:T(8,128)}, u32[]{:S(2)}) copy-start(f32[4096,64]{0,1:T(8,128)} %all-gather.4.cloned.1.call-done) | copy-start | bytes 3145732
  245.3 15.3 %copy-start.3 = (f32[1024,64]{0,1:T(8,128)}, f32[1024,64]{0,1:T(8,128)S(1)}, u32[]{:S(2)}) copy-start(f32[1024,64]{0,1:T(8,128)S(1)} %broadcast_multiply_fusion) | copy-start | bytes 786436
Sparse Core Ops, SparseCore 0:
  30.6 27.4 reduce-scatter.1
  61.5 71.0 all-reduce.1
  157.6 16.0 all-gather.3
  192.9 49.0 all-gather.5
